TPU v7x, 1024 devices: a whole 8x8x8 slice. The times are simulated.
1024 devices in a mesh: tpair: 128 (over z, x, core), col: 8 (over y).
Axes of the slice: x: 8, y: 8, z: 8, core: 2. Of those that a mesh axis runs over, the one named last changes fastest.
Arguments:
- peramb: bfloat16 [128, 2, 2048, 2048], P('tpair', None, None, 'col'), may hold values from -6 to 6
- sink_ops: bfloat16 [128, 2, 2, 512, 512], P('tpair'), may hold values from -0.1875 to 0.1875
- op_table: bfloat16 [2048, 2, 512], P('tpair'), may hold values from -0.1875 to 0.1875
- row_slot: int32 [2048], replicated, may hold values from 0 to 2047, each once
- pair_source: int32 [128], P('tpair'), may hold values from 0 to 1
- op_index: int32 [256, 2], P('tpair'), may hold values from 0 to 1
- listed_rows: int32 [256, 128], P('tpair'), may hold values from 0 to 511
Outputs:
- contracted: bfloat16 [256, 4, 128, 2, 2048], P('tpair', None, 'col')
Inputs may be any that keep to these rules, and one draw needn't show every extreme that they name: `row_slot`: every position of 0 to 2047 appears once.
All inputs are finite; a program needn't handle non-finite values.
Results may differ from a plain program's by a relative error of at most 0.0049.
Values may be sent and summed in bfloat16 or wider, within the bound.
A program may use at most 64 MiB of HBM per device.

v0:
```python
import jax
import jax.numpy as jnp
from jax import lax
from jax.sharding import PartitionSpec as P

NS = 4


def per_device(peramb, sink_ops, op_table, row_slot, pair_source, op_index, listed_rows):
    n_cols = lax.axis_size("col")
    eigen = op_table.shape[2]
    nops = sink_ops.shape[1]
    gathered = lax.all_gather(op_table, "tpair", axis=0, tiled=True)
    listed = listed_rows.shape[1]
    products = op_index.shape[0]
    left = sink_ops[0][op_index[:, 0:1], :, listed_rows]
    source_rows = (pair_source[0] * nops + op_index[:, 1:2]) * eigen
    right_pos = row_slot[source_rows + jnp.arange(eigen, dtype=jnp.int32)[None, :]]
    right = gathered[right_pos]
    left_re = left[:, :, 0]
    left_im = left[:, :, 1]
    left_block = jnp.stack([jnp.stack([left_re, -left_im], 2), jnp.stack([left_im, left_re], 2)], 1)
    local_cols = peramb.shape[3]
    spin_cols = peramb[0].reshape(2, NS, eigen, local_cols)
    mixed = jnp.einsum(
        "pjirv,rsvc->pjsic", left_block, spin_cols, preferred_element_type=jnp.float32
    )
    mixed = mixed.astype(jnp.bfloat16)
    own_rows = listed // n_cols
    order_full = NS * eigen
    right_re = right[:, :, 0]
    right_im = right[:, :, 1]
    right_block = jnp.stack(
        [jnp.stack([right_re, right_im], 2), jnp.stack([-right_im, right_re], 2)], 1
    )
    regrouped = lax.all_to_all(mixed, "col", split_axis=3, concat_axis=4, tiled=True)
    spins = regrouped.shape[2]
    split = regrouped.reshape(products, 2, spins, own_rows, NS, eigen)
    result = jnp.einsum(
        "pjsitv,pjvow->psiotw", split, right_block, preferred_element_type=jnp.float32
    )
    return result.reshape(products, spins, own_rows, 2, order_full).astype(jnp.bfloat16)


def solution(mesh):
    in_specs = (
        P("tpair", None, None, "col"),
        P("tpair", None, None, None, None),
        P("tpair", None, None),
        P(),
        P("tpair"),
        P("tpair", None),
        P("tpair", None),
    )
    out_specs = P("tpair", None, "col", None, None)
    return jax.shard_map(
        per_device, mesh=mesh, in_specs=in_specs, out_specs=out_specs, check_vma=False
    )
```

profile of v0, /device:TPU:113, one launch (start us, length us, event | category | flops | bytes accessed | tf_op | source)
XLA Modules:
  0.0 141.2 jit_solution(16278261658096917529)
XLA Ops:
  6.5 0.0 copy-start
  6.5 0.0 all-gather.2.cloned.1.call-start
  6.5 0.7 all-gather.2.cloned.1.call-update
  7.9 0.0 copy-start.3
  7.9 0.0 copy-start.4
  7.9 5.1 %copy.78 = bf16[1,2,2,512,512]{4,2,3,1,0:T(2,128)(2,1)} copy(bf16[1,2,2,512,512]{4,3,2,1,0:T(8,128)(2,1)} %param.8) | data formatting | bytes 4194304 | tf_op args[1]
  13.0 0.0 copy-done.3
  13.0 0.2 fusion.20
  13.2 0.0 copy-done.4
  13.2 0.1 fusion.19
  13.3 3.6 %gather_fusion.2 = bf16[256,2,512]{2,1,0:T(2,128)(2,1)S(1)} fusion(bf16[2,2,512,512]{3,1,2,0:T(2,128)(2,1)} %bitcast.92, s32[256]{0:T(256)S(1)} %fusion.19), kind=kCustom, calls=%fused_computation.2 | custom fusion | bytes 1050624 | tf_op jit(solution)/shard_map/gather | solution.py:16
  16.9 0.1 copy.44
  17.0 0.1 maximum_bitcast_fusion.7
  17.1 0.0 copy-done
  17.1 1.2 fusion.4
  18.4 0.0 copy-start.1
  18.4 1.8 %copy.49 = bf16[2,2,4,128,256]{4,2,1,0,3:T(4,128)(2,1)} copy(bf16[2,2,4,128,256]{4,3,2,1,0:T(8,128)(2,1)S(1)} %fusion.4) | data formatting | bytes 2097152 | tf_op jit(solution)/shard_map/convert_element_type | solution.py:28
  20.2 6.0 %all-to-all-start = ((bf16[2,2,4,128,256]{4,2,1,0,3:T(4,128)(2,1)}), bf16[2,2,4,128,256]{4,2,1,0,3:T(4,128)(2,1)S(1)}, u32[]{:S(2)}, u32[]{:S(2)}) async-start(bf16[2,2,4,128,256]{4,2,1,0,3:T(4,128)(2,1)} %copy.49), calls=%async_computation | async-start | bytes 2097152 | tf_op jit(solution)/shard_map/all_to_all | solution.py:36
  26.2 0.1 fusion.11
  26.2 0.0 copy-done.1
  26.3 6.2 %gather_fusion = s32[1024]{0:T(1024)S(1)} fusion(s32[2048]{0:T(1024)S(1)} %copy-done.1, s32[1024]{0:T(1024)S(1)} %broadcast_clamp_fusion), kind=kCustom, calls=%fused_computation | custom fusion | bytes 12288 | tf_op jit(solution)/shard_map/gather | solution.py:18
  32.5 5.7 %all-to-all-done = bf16[2,2,4,128,256]{4,2,1,0,3:T(4,128)(2,1)S(1)} async-done(((bf16[2,2,4,128,256]{4,2,1,0,3:T(4,128)(2,1)}), bf16[2,2,4,128,256]{4,2,1,0,3:T(4,128)(2,1)S(1)}, u32[]{:S(2)}, u32[]{:S(2)}) %all-to-all-start) | async-done | bytes 1048608 | tf_op jit(solution)/shard_map/all_to_all | solution.py:36
  38.1 1.6 %copy.79 = bf16[2,2,4,8,16,256]{5,3,4,2,1,0:T(8,128)(2,1)} copy(bf16[2,2,4,8,16,256]{5,2,1,0,4,3:T(4,128)(2,1)S(1)} %bitcast.90) | data formatting | bytes 2097152 | tf_op jit(solution)/shard_map/all_to_all | solution.py:36
  39.7 1.7 %reshape.66 = bf16[2,2,4,16,4,512]{5,4,3,2,1,0:T(4,128)(2,1)S(1)} reshape(bf16[2,2,4,16,8,256]{5,4,3,2,1,0:T(8,128)(2,1)} %bitcast.91) | data formatting | bytes 2097152 | tf_op jit(solution)/shard_map/reshape | solution.py:38
  41.4 72.4 %all-gather.2.cloned.1.call-done = bf16[2048,2,512]{2,1,0:T(2,128)(2,1)} async-done(((bf16[16,2,512]{2,1,0:T(2,128)(2,1)}), bf16[2048,2,512]{2,1,0:T(2,128)(2,1)}) %all-gather.2.cloned.1.call-update) | async-done | bytes 4194320 | tf_op jit(solution)/shard_map/all_gather | solution.py:13
  113.8 13.1 %gather_fusion.1 = bf16[1024,2,512]{2,1,0:T(2,128)(2,1)} fusion(bf16[2048,2,512]{2,1,0:T(2,128)(2,1)} %all-gather.2.cloned.1.call-done, s32[1024]{0:T(1024)S(1)} %broadcast_clamp_fusion.1), kind=kCustom, calls=%fused_computation.1 | custom fusion | bytes 4198400 | tf_op jit(solution)/shard_map/gather | solution.py:19
  127.0 1.9 %copy.39 = bf16[1024,2,512]{2,0,1:T(8,128)(2,1)S(1)} copy(bf16[1024,2,512]{2,1,0:T(2,128)(2,1)} %gather_fusion.1) | data formatting | bytes 4194304 | tf_op jit(solution)/shard_map/gather | solution.py:19
  128.9 0.0 copy-start.2
  128.9 0.1 fusion.5
  129.0 0.1 slice_bitcast_fusion
  129.1 1.4 %copy-done.2 = bf16[1024,2,512]{2,1,0:T(2,128)(2,1)S(1)} copy-done((bf16[1024,2,512]{2,1,0:T(2,128)(2,1)S(1)}, bf16[1024,2,512]{2,1,0:T(2,128)(2,1)}, u32[]{:S(2)}) %copy-start.2) | copy-done | bytes 2097176
  130.5 0.4 copy.42
  130.8 0.2 maximum_bitcast_fusion.2
  131.0 1.2 fusion.3
  132.3 0.8 copy.66
  133.1 1.2 reshape.109
  (8 shorter events, 0.1 us)
Async XLA Ops:
  6.5 10.6 %copy-start = (bf16[1,2,2048,256]{3,2,1,0:T(8,128)(2,1)S(1)}, bf16[1,2,2048,256]{3,2,1,0:T(8,128)(2,1)}, u32[]{:S(2)}) copy-start(bf16[1,2,2048,256]{3,2,1,0:T(8,128)(2,1)} %param.7) | copy-start | bytes 6291460
  6.5 107.3 %all-gather.2.cloned.1.call-start = ((), (), s32[]{:S(2)}) async-start(), calls=%async_computation.1 | async-start | bytes 4227072 | tf_op jit(solution)/shard_map/all_gather | solution.py:13
  7.9 5.1 %copy-start.3 = (s32[2,2]{1,0:T(2,128)S(1)}, s32[2,2]{1,0:T(2,128)}, u32[]{:S(2)}) copy-start(s32[2,2]{1,0:T(2,128)} %param.12) | copy-start | bytes 52
  7.9 5.3 %copy-start.4 = (s32[2,128]{1,0:T(2,128)S(1)}, s32[2,128]{1,0:T(2,128)}, u32[]{:S(2)}) copy-start(s32[2,128]{1,0:T(2,128)} %param.13) | copy-start | bytes 3076
  18.4 7.8 %copy-start.1 = (s32[2048]{0:T(1024)S(1)}, s32[2048]{0:T(1024)}, u32[]{:S(2)}) copy-start(s32[2048]{0:T(1024)} %param.10) | copy-start | bytes 24580
  20.2 17.9 %all-to-all-start = ((bf16[2,2,4,128,256]{4,2,1,0,3:T(4,128)(2,1)}), bf16[2,2,4,128,256]{4,2,1,0,3:T(4,128)(2,1)S(1)}, u32[]{:S(2)}, u32[]{:S(2)}) async-start(bf16[2,2,4,128,256]{4,2,1,0,3:T(4,128)(2,1)} %copy.49), calls=%async_computation | async-start | bytes 2097152 | tf_op jit(solution)/shard_map/all_to_all | solution.py:36
  128.9 1.6 %copy-start.2 = (bf16[1024,2,512]{2,1,0:T(2,128)(2,1)S(1)}, bf16[1024,2,512]{2,1,0:T(2,128)(2,1)}, u32[]{:S(2)}) copy-start(bf16[1024,2,512]{2,1,0:T(2,128)(2,1)} %gather_fusion.1) | copy-start | bytes 6291460
Sparse Core Ops, SparseCore 0:
  11.6 102.1 all-gather.1
where the time goes:
time: 144 us; the launch traced here: 141 us
  waiting for transfers between devices  78.8 us (55%)
  local copies, waits for them, and re-layouts  39 us (27%)
  between operations  14.2 us (10%)
  starting transfers between devices  5.97 us (4%)
  matrix products  2.49 us (2%)
    all_gather x1, waiting for transfers between devices, per_device(): gathered = lax.all_gather(op_table, 'tpair', axis=0, tiled=True)  72.4 us
    gather x2, local copies, waits for them, and re-layouts, per_device(): right = gathered[right_pos]  15.1 us
    unnamed x15, local copies, waits for them, and re-layouts  6.65 us
    gather x2, local copies, waits for them, and re-layouts, per_device(): row_slot[source_rows + jnp.arange(eigen, dtype=jnp.int32)[None, :]]  6.16 us
    all_to_all x1, starting transfers between devices, per_device(): lax.all_to_all(mixed, 'col', split_axis=3, concat_axis=4, tiled=True)  5.97 us
    all_to_all x1, waiting for transfers between devices, per_device(): lax.all_to_all(mixed, 'col', split_axis=3, concat_axis=4, tiled=True)  5.66 us
    gather x2, local copies, waits for them, and re-layouts, per_device(): left = sink_ops[0][op_index[:, 0:1], :, listed_rows]  3.69 us
  transfers between devices with their start and end apart: 2, of which 2 were waited for; matrix products, arithmetic and copies ran while one was open for 15% of the time, Pallas kernels for 0%

commit v1 on v0

v1 whole, which is shorter than its diff:
```python
import jax
import jax.numpy as jnp
from jax import lax
from jax.experimental import pallas as pl
from jax.experimental.pallas import tpu as pltpu
from jax.sharding import PartitionSpec as P

NS = 4
CORES = 2
SIDE = 8
MESH = pl.DeviceIdType.MESH
BF16 = jnp.bfloat16
F32 = jnp.float32


def column_of(row):
    n = row.shape[1]
    return jnp.transpose(jnp.broadcast_to(row, (n, n)))


def onehot_rows(row, width, base=0):
    col = column_of(row)
    n = col.shape[0]
    lane = lax.broadcasted_iota(jnp.int32, (n, n), 1) + base
    parts = [(col == lane + w * n).astype(F32).astype(BF16) for w in range(width // n)]
    return jnp.concatenate(parts, axis=1)


def kernel(
    source_ref, op_ref, listed_ref, slot_ref, peramb_ref, sink_ref, optab_ref, out_ref,
    perv, sinkv, lhs, sendb, recvb, tbl, hot, right, outv,
    in_sem, out_sem, a2a_send, a2a_recv, p1_send, p1_recv, p2_send, p2_recv, fw_send, fw_recv,
):
    nv = sinkv.shape[3]
    n_y = sendb.shape[1]
    own = sendb.shape[2] // (2 * CORES)
    prods = op_ref.shape[0]
    sel = listed_ref.shape[1]
    n = SIDE
    half = n // 2
    t = lax.axis_index("tpair")
    y = lax.axis_index("col")
    c = t % CORES
    x = (t // CORES) % n
    z = t // (CORES * n)
    a = (1 - c) * z + c * x
    b = (1 - c) * x + c * z
    partner = (t + 1 - 2 * c, y)

    def ring_id(a_, b_):
        z_ = (1 - c) * a_ + c * b_
        x_ = (1 - c) * b_ + c * a_
        return ((z_ * n + x_) * CORES + c, y)

    loads = [pltpu.make_async_copy(sink_ref.at[0], sinkv, in_sem.at[0])]
    for s in range(NS):
        for r in range(2):
            loads.append(
                pltpu.make_async_copy(
                    peramb_ref.at[0, r, pl.ds(s * nv, nv)], perv.at[s, r], in_sem.at[1 + s * 2 + r]
                )
            )
    for cp in loads:
        cp.start()

    barrier = pltpu.get_barrier_semaphore()
    peers = [(t, (y + i) % n_y) for i in range(1, n_y)]
    peers += [ring_id(a, (b + i) % n) for i in range(1, n)]
    peers += [ring_id((a + 1) % n, b), ring_id((a + n - 1) % n, b), partner]
    for dev in peers:
        pl.semaphore_signal(barrier, inc=1, device_id=dev, device_id_type=MESH)

    shard = optab_ref[...].astype(F32)
    for r in range(2):
        tbl[c, a, b, r] = shard[:, r, :].astype(BF16)

    row = lax.broadcasted_iota(jnp.int32, (2 * sel, sel), 0)
    col = lax.broadcasted_iota(jnp.int32, (2 * sel, sel), 1)
    even = (row == 2 * col).astype(F32)
    odd = (row == 2 * col + 1).astype(F32)
    spread_a = jnp.concatenate([even, odd], axis=1).astype(BF16)
    spread_b = jnp.concatenate([odd, -even], axis=1).astype(BF16)
    hots = [onehot_rows(listed_ref[k : k + 1, :], nv) for k in range(prods)]
    loads[0].wait()
    for k in range(prods):
        ops = sinkv[op_ref[k, 0]]
        g_re = jnp.dot(hots[k], ops[0], preferred_element_type=F32).astype(BF16)
        g_im = jnp.dot(hots[k], ops[1], preferred_element_type=F32).astype(BF16)
        g = jnp.concatenate([g_re, g_im], axis=0)
        left_a = jnp.dot(spread_a, g, preferred_element_type=F32).astype(BF16)
        left_b = jnp.dot(spread_b, g, preferred_element_type=F32).astype(BF16)
        lhs[:, k, :, 0:nv] = left_a.reshape(n_y, 2 * own, nv)
        lhs[:, k, :, nv : 2 * nv] = left_b.reshape(n_y, 2 * own, nv)

    pl.semaphore_wait(barrier, len(peers))

    phase1 = []
    for i in range(1, n):
        phase1.append(
            pltpu.make_async_remote_copy(
                src_ref=tbl.at[c, a, b], dst_ref=tbl.at[c, a, b],
                send_sem=p1_send.at[i], recv_sem=p1_recv.at[i],
                device_id=ring_id(a, (b + i) % n), device_id_type=MESH,
            )
        )
    for cp in phase1:
        cp.start()

    exchange = []
    for s in range(NS):
        loads[1 + 2 * s].wait()
        loads[2 + 2 * s].wait()
        m = jnp.dot(
            lhs[...].reshape(n_y * prods * 2 * own, 2 * nv),
            perv[s].reshape(2 * nv, perv.shape[3]),
            preferred_element_type=F32,
        )
        sendb[s] = m.astype(BF16).reshape(sendb.shape[1:])
        recvb[s, y] = sendb[s, y]
        for i in range(1, n_y):
            dest = (y + i) % n_y
            cp = pltpu.make_async_remote_copy(
                src_ref=sendb.at[s, dest], dst_ref=recvb.at[s, y],
                send_sem=a2a_send.at[s, i], recv_sem=a2a_recv.at[s, i],
                device_id=(t, dest), device_id_type=MESH,
            )
            cp.start()
            exchange.append(cp)

    for k in range(prods):
        first = source_ref[0] * prods + op_ref[k, 1]
        pos = slot_ref[first]
        pt = pos // 16
        pr = pos % 16
        pc = pt % CORES
        px = (pt // CORES) % n
        pz = pt // (CORES * n)
        pa = (1 - pc) * pz + pc * px
        pb = (1 - pc) * px + pc * pz
        idx = ((pc * n + pa) * n + pb) * 16 + pr
        for j in range(nv // 128):
            hot[pl.ds(k * nv + j * 128, 128), :] = onehot_rows(idx[j : j + 1, :], hot.shape[1])

    for cp in phase1:
        cp.wait_recv()

    plus = ring_id((a + 1) % n, b)
    minus = ring_id((a + n - 1) % n, b)
    phase2 = {}
    forward = {}

    def hop(d, st, h):
        block = (a + n - st + 1) % n if d == 0 else (a + st - 1) % n
        part = tbl.at[c, block, pl.ds(h * half, half)]
        cp = pltpu.make_async_remote_copy(
            src_ref=part, dst_ref=part,
            send_sem=p2_send.at[d, st, h], recv_sem=p2_recv.at[d, st, h],
            device_id=plus if d == 0 else minus, device_id_type=MESH,
        )
        cp.start()
        phase2[d, st, h] = cp

    def pass_on(d, st, h):
        block = (a + n - st) % n if d == 0 else (a + st) % n
        part = tbl.at[c, block, pl.ds(h * half, half)]
        cp = pltpu.make_async_remote_copy(
            src_ref=part, dst_ref=part,
            send_sem=fw_send.at[d, st, h], recv_sem=fw_recv.at[d, st, h],
            device_id=partner, device_id_type=MESH,
        )
        cp.start()
        forward[d, st, h] = cp

    for h in range(2):
        for d in range(2):
            if half > 1 or h == d:
                hop(d, 1, h)
    for h in range(2):
        pass_on(0, 0, h)
    for st in range(1, half + 1):
        for h in range(2):
            for d in range(2):
                if (d, st, h) in phase2:
                    phase2[d, st, h].wait_recv()
                    if st + 1 < half or (st + 1 == half and h == d):
                        hop(d, st + 1, h)
                    pass_on(d, st, h)
    for cp in forward.values():
        cp.wait_recv()

    slots = hot.shape[1]

    def pick(j, carry):
        r = j // 2
        at = pl.ds(pl.multiple_of((j % 2) * (nv // 2), nv // 2), nv // 2)
        rows = tbl[:, :, :, r, :, at].reshape(slots, nv // 2)
        got = jnp.dot(hot[...], rows, preferred_element_type=F32).astype(BF16)
        right[:, :, pl.ds(pl.multiple_of(j * (nv // 2), nv // 2), nv // 2)] = got.reshape(
            prods, nv, nv // 2
        )
        return carry

    lax.fori_loop(0, 4, pick, 0)

    rows = NS * 2 * own
    parity = lax.broadcasted_iota(jnp.int32, (rows, nv), 0) % 2
    stores = []
    per_t = n_y // NS
    for s in range(NS):
        for i in range(1, n_y):
            exchange[s * (n_y - 1) + i - 1].wait_recv()
        for k in range(prods):
            got = recvb[s].reshape(NS, per_t, prods * 2 * own, nv // per_t)
            mixed = jnp.concatenate(
                [
                    got[:, h, k * 2 * own : (k + 1) * 2 * own, :].reshape(rows, nv // per_t)
                    for h in range(per_t)
                ],
                axis=1,
            )
            both = jnp.dot(mixed, right[k], preferred_element_type=F32)
            by_re = both[:, :nv]
            by_im = both[:, nv:]
            turned = jnp.where(
                parity == 0, -pltpu.roll(by_im, rows - 1, 0), pltpu.roll(by_im, 1, 0)
            )
            res = (by_re + turned).astype(BF16)
            for tt in range(NS):
                outv[k, s, :, tt * nv : (tt + 1) * nv] = res[tt * 2 * own : (tt + 1) * 2 * own]
            cp = pltpu.make_async_copy(outv.at[k, s], out_ref.at[k, s], out_sem.at[k, s])
            cp.start()
            stores.append(cp)

    for cp in phase1 + exchange + list(phase2.values()) + list(forward.values()):
        cp.wait_send()
    for cp in stores:
        cp.wait()


def per_device(peramb, sink_ops, op_table, row_slot, pair_source, op_index, listed_rows):
    n_y = lax.axis_size("col")
    nv = op_table.shape[2]
    cols = peramb.shape[3]
    prods, sel = listed_rows.shape
    own = sel // n_y
    shard = op_table.shape[0]
    order = NS * nv
    slots = lax.axis_size("tpair") * shard
    half = SIDE // 2
    dma = pltpu.SemaphoreType.DMA
    vmem = pl.BlockSpec(memory_space=pltpu.VMEM)
    smem = pl.BlockSpec(memory_space=pltpu.SMEM)
    hbm = pl.BlockSpec(memory_space=pl.ANY)
    out = pl.pallas_call(
        kernel,
        out_shape=jax.ShapeDtypeStruct((prods, NS, 2 * own, order), BF16),
        in_specs=[smem, smem, vmem, vmem, hbm, hbm, vmem],
        out_specs=hbm,
        scratch_shapes=[
            pltpu.VMEM((NS, 2, nv, cols), BF16),
            pltpu.VMEM(sink_ops.shape[1:], BF16),
            pltpu.VMEM((n_y, prods, 2 * own, 2 * nv), BF16),
            pltpu.VMEM((NS, n_y, prods * 2 * own, cols), BF16),
            pltpu.VMEM((NS, n_y, prods * 2 * own, cols), BF16),
            pltpu.VMEM((CORES, SIDE, SIDE, 2, shard, nv), BF16),
            pltpu.VMEM((prods * nv, slots), BF16),
            pltpu.VMEM((prods, nv, 2 * nv), BF16),
            pltpu.VMEM((prods, NS, 2 * own, order), BF16),
            dma((1 + 2 * NS,)),
            dma((prods, NS)),
            dma((NS, n_y)),
            dma((NS, n_y)),
            dma((SIDE,)),
            dma((SIDE,)),
            dma((2, half + 1, 2)),
            dma((2, half + 1, 2)),
            dma((2, half + 1, 2)),
            dma((2, half + 1, 2)),
        ],
        compiler_params=pltpu.CompilerParams(
            collective_id=0, has_side_effects=True, vmem_limit_bytes=56 << 20
        ),
        name="contract",
    )(
        pair_source,
        op_index,
        listed_rows,
        row_slot.reshape(-1, nv // 128, 128),
        peramb,
        sink_ops,
        op_table,
    )
    return out.reshape(prods, NS, own, 2, order)


def solution(mesh):
    in_specs = (
        P("tpair", None, None, "col"),
        P("tpair", None, None, None, None),
        P("tpair", None, None),
        P(),
        P("tpair"),
        P("tpair", None),
        P("tpair", None),
    )
    out_specs = P("tpair", None, "col", None, None)
    return jax.shard_map(
        per_device, mesh=mesh, in_specs=in_specs, out_specs=out_specs, check_vma=False
    )
```

time: 144 us -> 63.2 us (0.44)
  the two profiles are of different devices: /device:TPU:113 before, /device:TPU:1 now
where the time goes in v1:
time: 63.2 us; the launch traced here: 63 us
  Pallas kernels  59.8 us (95%)
  local copies, waits for them, and re-layouts  2.53 us (4%)
  between operations  0.66 us (1%)
    pallas_call x1, Pallas kernels, per_device(): pl.pallas_call(kernel, out_shape=jax.ShapeDtypeStruct((prods, NS, 2 * own...  59.8 us
    reshape x1, local copies, waits for them, and re-layouts, per_device(): return out.reshape(prods, NS, own, 2, order)  2.53 us

profile of v1, /device:TPU:1, one launch (start us, length us, event | category | flops | bytes accessed | tf_op | source)
XLA Modules:
  0.0 63.0 jit_solution(688491750201996648)
XLA Ops:
  0.7 59.8 %contract.1 = bf16[2,4,32,2048]{3,2,1,0:T(8,128)(2,1)} custom-call(s32[1]{0:T(128)S(6)} %copy.8.source_ref, s32[2,2]{1,0:T(2,128)} %op_ref.1, s32[2,128]{1,0:T(2,128)} %listed_ref.1, s32[4,4,128]{2,1,0:T(4,128)} %bitcast.3, bf16[1,2,2048,256]{3,2,1,0:T(8,128)(2,1)} %peramb_ref.1, bf16[1,2,2,512,512]{4,3,2,1,0:T(8,128)(2,1)} %sink_ref.1, ...), custom_call_target="tpu_custom_call" | custom-call | tf_op jit(solution)/shard_map/contract/pallas_call | solution.py:254
  60.4 2.5 %reshape.7 = bf16[2,4,16,2,2048]{4,3,2,1,0:T(2,128)(2,1)} reshape(bf16[2,4,32,2048]{3,2,1,0:T(8,128)(2,1)} %contract.1) | data formatting | bytes 2097152 | tf_op jit(solution)/shard_map/reshape | solution.py:293

commit v2 on v1

v2 whole, which is shorter than its diff:
```python
import jax
import jax.numpy as jnp
from jax import lax
from jax.experimental import pallas as pl
from jax.experimental.pallas import tpu as pltpu
from jax.sharding import PartitionSpec as P

NS = 4
CORES = 2
SIDE = 8
MESH = pl.DeviceIdType.MESH
BF16 = jnp.bfloat16
F32 = jnp.float32


def column_of(row):
    n = row.shape[1]
    return jnp.transpose(jnp.broadcast_to(row, (n, n)))


def onehot_rows(row, width, base=0):
    col = column_of(row)
    n = col.shape[0]
    lane = lax.broadcasted_iota(jnp.int32, (n, n), 1) + base
    parts = [(col == lane + w * n).astype(F32).astype(BF16) for w in range(width // n)]
    return jnp.concatenate(parts, axis=1)


def kernel(
    source_ref, op_ref, listed_ref, slot_ref, peramb_ref, sink_ref, optab_ref, out_ref,
    perv, sinkv, lhs, sendb, recvb, tbl, hot, right,
    in_sem, a2a_send, a2a_recv, p1_send, p1_recv, hop_send, hop_recv, fw_send, fw_recv,
    ready_y, ready_z, ready_x, ready_c,
):
    nv = sinkv.shape[3]
    n_y = sendb.shape[1]
    own = sendb.shape[2] // (2 * CORES)
    prods = op_ref.shape[0]
    sel = listed_ref.shape[1]
    n = SIDE
    half = n // 2
    quarters = n // 2
    t = lax.axis_index("tpair")
    y = lax.axis_index("col")
    c = t % CORES
    x = (t // CORES) % n
    z = t // (CORES * n)

    def at_z(i):
        return ((((z + i) % n) * n + x) * CORES + c, y)

    def at_x(i):
        return ((z * n + (x + i) % n) * CORES + c, y)

    def at_y(i):
        return (t, (y + i) % n_y)

    partner = (t + 1 - 2 * c, y)

    loads = [pltpu.make_async_copy(sink_ref.at[0], sinkv, in_sem.at[0])]
    for s in range(NS):
        for r in range(2):
            loads.append(
                pltpu.make_async_copy(
                    peramb_ref.at[0, r, pl.ds(s * nv, nv)], perv.at[s, r], in_sem.at[1 + s * 2 + r]
                )
            )
    for cp in loads:
        cp.start()

    peers = []
    for i in range(1, n_y):
        peers.append((at_y(i), y + i < n_y, ready_y.at[i], ready_y.at[n_y - i]))
    for i in range(1, n):
        peers.append((at_z(i), z + i < n, ready_z.at[i], ready_z.at[n - i]))
    for i in (1, n - 1):
        peers.append((at_x(i), x + i < n, ready_x.at[i], ready_x.at[n - i]))
    peers.append((partner, c == 1, ready_c.at[0], ready_c.at[0]))
    barrier = pltpu.get_barrier_semaphore()
    for dev, later, _, _ in peers:

        @pl.when(later)
        def _(dev=dev):
            pl.semaphore_signal(barrier, inc=1, device_id=dev, device_id_type=MESH)

    shard = optab_ref[...].astype(F32)
    for r in range(2):
        tbl[z, x, c, r] = shard[:, r, :].astype(BF16)

    earlier = y + z + (x + n - 1) // n + (x + 1) // n + 1 - c

    @pl.when(earlier > 0)
    def _():
        pl.semaphore_wait(barrier, earlier)

    for dev, later, _, theirs in peers:

        @pl.when(jnp.logical_not(later))
        def _(dev=dev, theirs=theirs):
            pl.semaphore_signal(theirs, inc=1, device_id=dev, device_id_type=MESH)

    def await_answer(index):
        _, later, mine, _ = peers[index]

        @pl.when(later)
        def _():
            pl.semaphore_wait(mine, 1)

    def shard_copy(i):
        return pltpu.make_async_remote_copy(
            src_ref=tbl.at[z, x, c], dst_ref=tbl.at[z, x, c],
            send_sem=p1_send.at[i], recv_sem=p1_recv.at[i],
            device_id=at_z(i), device_id_type=MESH,
        )

    phase1 = [None] + [shard_copy(i) for i in range(1, n)]
    for i in range(1, n):

        @pl.when(z + i >= n)
        def _(i=i):
            phase1[i].start()

    row = lax.broadcasted_iota(jnp.int32, (2 * sel, sel), 0)
    col = lax.broadcasted_iota(jnp.int32, (2 * sel, sel), 1)
    even = (row == 2 * col).astype(F32)
    odd = (row == 2 * col + 1).astype(F32)
    spread_a = jnp.concatenate([even, odd], axis=1).astype(BF16)
    spread_b = jnp.concatenate([odd, -even], axis=1).astype(BF16)
    hots = [onehot_rows(listed_ref[k : k + 1, :], nv) for k in range(prods)]
    loads[0].wait()
    for k in range(prods):
        ops = sinkv[op_ref[k, 0]]
        g_re = jnp.dot(hots[k], ops[0], preferred_element_type=F32).astype(BF16)
        g_im = jnp.dot(hots[k], ops[1], preferred_element_type=F32).astype(BF16)
        g = jnp.concatenate([g_re, g_im], axis=0)
        left_a = jnp.dot(spread_a, g, preferred_element_type=F32).astype(BF16)
        left_b = jnp.dot(spread_b, g, preferred_element_type=F32).astype(BF16)
        lhs[:, k, :, 0:nv] = left_a.reshape(n_y, 2 * own, nv)
        lhs[:, k, :, nv : 2 * nv] = left_b.reshape(n_y, 2 * own, nv)

    exchange = []
    for s in range(NS):
        loads[1 + 2 * s].wait()
        loads[2 + 2 * s].wait()
        m = jnp.dot(
            lhs[...].reshape(n_y * prods * 2 * own, 2 * nv),
            perv[s].reshape(2 * nv, perv.shape[3]),
            preferred_element_type=F32,
        )
        sendb[s] = m.astype(BF16).reshape(sendb.shape[1:])
        recvb[s, y] = sendb[s, y]
        for i in range(1, n_y):
            if s == 0:
                await_answer(i - 1)
            cp = pltpu.make_async_remote_copy(
                src_ref=sendb.at[s, (y + i) % n_y], dst_ref=recvb.at[s, y],
                send_sem=a2a_send.at[s, i], recv_sem=a2a_recv.at[s, i],
                device_id=at_y(i), device_id_type=MESH,
            )
            cp.start()
            exchange.append(cp)

    for k in range(prods):
        pos = slot_ref[source_ref[0] * prods + op_ref[k, 1]]
        for j in range(nv // 128):
            hot[pl.ds(k * nv + j * 128, 128), :] = onehot_rows(pos[j : j + 1, :], hot.shape[1])

    hops = {}
    forward = {}

    def piece(q, d, st, block):
        if st < half:
            return tbl.at[pl.ds(2 * q, 2), block, c]
        return tbl.at[pl.ds(2 * q + d, 1), block, c]

    def hop(q, d, st):
        part = piece(q, d, st, (x + n - st + 1) % n if d == 0 else (x + st - 1) % n)
        cp = pltpu.make_async_remote_copy(
            src_ref=part, dst_ref=part,
            send_sem=hop_send.at[q, d, st], recv_sem=hop_recv.at[q, d, st],
            device_id=at_x(1 if d == 0 else n - 1), device_id_type=MESH,
        )
        cp.start()
        hops[q, d, st] = cp

    def pass_on(q, d, st):
        part = piece(q, d, st, (x + n - st) % n if d == 0 else (x + st) % n)
        cp = pltpu.make_async_remote_copy(
            src_ref=part, dst_ref=part,
            send_sem=fw_send.at[q, d, st], recv_sem=fw_recv.at[q, d, st],
            device_id=partner, device_id_type=MESH,
        )
        cp.start()
        forward[q, d, st] = cp

    def open_pair(q):
        for w in (2 * q, 2 * q + 1):
            for i in range(1, n):
                if i <= w:

                    @pl.when(z + i == w)
                    def _(i=i):
                        pl.semaphore_wait(ready_z.at[i], 1)
                        phase1[i].start()

        for w in (2 * q, 2 * q + 1):
            for i in range(1, n):

                @pl.when((w + i) % n == z)
                def _(i=i):
                    phase1[i].wait_recv()

        if q == 0:
            await_answer(n_y - 1 + n - 1)
            await_answer(n_y - 1 + n)
        for d in range(2):
            hop(q, d, 1)
        if q == 0:
            await_answer(n_y - 1 + n + 1)
        pass_on(q, 0, 0)

    def relay(q, st):
        for d in range(2):
            hops[q, d, st].wait_recv()
            if st < half:
                hop(q, d, st + 1)
            pass_on(q, d, st)

    def pick(q):
        for d in range(2):
            for st in range(half + 1):
                if (q, d, st) in forward:
                    forward[q, d, st].wait_recv()
        span = hot.shape[1] // quarters
        width = nv // 2

        def column(j, carry):
            at = pl.ds(pl.multiple_of((j % 2) * width, width), width)
            rows = tbl[2 * q : 2 * q + 2, :, :, j // 2, :, at].reshape(span, width)
            got = jnp.dot(
                hot[:, q * span : (q + 1) * span], rows, preferred_element_type=F32
            ).astype(BF16).reshape(prods, nv, width)
            to = pl.ds(pl.multiple_of(j * width, width), width)
            if q == 0:
                right[:, :, to] = got
            else:
                right[:, :, to] = right[:, :, to] + got
            return carry

        lax.fori_loop(0, 4, column, 0)

    open_pair(0)
    relay(0, 1)
    relay(0, 2)
    open_pair(1)
    relay(0, 3)
    relay(1, 1)
    relay(0, 4)
    relay(1, 2)
    pick(0)
    open_pair(2)
    relay(1, 3)
    relay(2, 1)
    open_pair(3)
    relay(1, 4)
    relay(2, 2)
    pick(1)
    relay(3, 1)
    relay(2, 3)
    relay(3, 2)
    relay(2, 4)
    pick(2)
    relay(3, 3)
    relay(3, 4)
    pick(3)

    for cp in exchange:
        cp.wait_recv()
    per_t = n_y // NS
    group = NS // 2
    rows = group * NS * 2 * own
    parity = lax.broadcasted_iota(jnp.int32, (rows, nv), 0) % 2
    for k in range(prods):
        for m in range(2):
            got = recvb[m * group : (m + 1) * group].reshape(
                group * NS, per_t, prods * 2 * own, nv // per_t
            )
            mixed = jnp.concatenate(
                [
                    got[:, h, k * 2 * own : (k + 1) * 2 * own, :].reshape(rows, nv // per_t)
                    for h in range(per_t)
                ],
                axis=1,
            )
            both = jnp.dot(mixed, right[k], preferred_element_type=F32)
            by_re = both[:, :nv]
            by_im = both[:, nv:]
            turned = jnp.where(
                parity == 0, -pltpu.roll(by_im, rows - 1, 0), pltpu.roll(by_im, 1, 0)
            )
            res = (by_re + turned).astype(BF16).reshape(group, NS, 2 * own, nv)
            for tt in range(NS):
                out_ref[k, m * group : (m + 1) * group, :, tt * nv : (tt + 1) * nv] = res[:, tt]

    for cp in phase1[1:] + exchange + list(hops.values()) + list(forward.values()):
        cp.wait_send()


def per_device(peramb, sink_ops, op_table, row_slot, pair_source, op_index, listed_rows):
    n_y = lax.axis_size("col")
    nv = op_table.shape[2]
    cols = peramb.shape[3]
    prods, sel = listed_rows.shape
    own = sel // n_y
    shard = op_table.shape[0]
    order = NS * nv
    slots = lax.axis_size("tpair") * shard
    half = SIDE // 2
    dma = pltpu.SemaphoreType.DMA
    vmem = pl.BlockSpec(memory_space=pltpu.VMEM)
    smem = pl.BlockSpec(memory_space=pltpu.SMEM)
    hbm = pl.BlockSpec(memory_space=pl.ANY)
    out = pl.pallas_call(
        kernel,
        out_shape=pltpu.VMEM((prods, NS, 2 * own, order), BF16),
        in_specs=[smem, smem, vmem, vmem, hbm, hbm, vmem],
        out_specs=vmem,
        scratch_shapes=[
            pltpu.VMEM((NS, 2, nv, cols), BF16),
            pltpu.VMEM(sink_ops.shape[1:], BF16),
            pltpu.VMEM((n_y, prods, 2 * own, 2 * nv), BF16),
            pltpu.VMEM((NS, n_y, prods * 2 * own, cols), BF16),
            pltpu.VMEM((NS, n_y, prods * 2 * own, cols), BF16),
            pltpu.VMEM((SIDE, SIDE, CORES, 2, shard, nv), BF16),
            pltpu.VMEM((prods * nv, slots), BF16),
            pltpu.VMEM((prods, nv, 2 * nv), BF16),
            dma((1 + 2 * NS,)),
            dma((NS, n_y)),
            dma((NS, n_y)),
            dma((SIDE,)),
            dma((SIDE,)),
            dma((half, 2, half + 1)),
            dma((half, 2, half + 1)),
            dma((half, 2, half + 1)),
            dma((half, 2, half + 1)),
            pltpu.SemaphoreType.REGULAR((n_y,)),
            pltpu.SemaphoreType.REGULAR((SIDE,)),
            pltpu.SemaphoreType.REGULAR((SIDE,)),
            pltpu.SemaphoreType.REGULAR((1,)),
        ],
        compiler_params=pltpu.CompilerParams(
            collective_id=0, has_side_effects=True, vmem_limit_bytes=56 << 20
        ),
        name="contract",
    )(
        pair_source,
        op_index,
        listed_rows,
        row_slot.reshape(-1, nv // 128, 128),
        peramb,
        sink_ops,
        op_table,
    )
    return out.reshape(prods, NS, own, 2, order)


def solution(mesh):
    in_specs = (
        P("tpair", None, None, "col"),
        P("tpair", None, None, None, None),
        P("tpair", None, None),
        P(),
        P("tpair"),
        P("tpair", None),
        P("tpair", None),
    )
    out_specs = P("tpair", None, "col", None, None)
    return jax.shard_map(
        per_device, mesh=mesh, in_specs=in_specs, out_specs=out_specs, check_vma=False
    )
```

time: 63.2 us -> 96.9 us (1.53)
  the two profiles are of different devices: /device:TPU:1 before, /device:TPU:769 now
where the time goes in v2:
time: 96.9 us; the launch traced here: 96.7 us
  Pallas kernels  94.6 us (98%)
  local copies, waits for them, and re-layouts  1.5 us (2%)
    pallas_call x1, Pallas kernels, per_device(): pl.pallas_call(kernel, out_shape=pltpu.VMEM((prods, NS, 2 * own, order),...  94.6 us

profile of v2, /device:TPU:769, one launch (start us, length us, event | category | flops | bytes accessed | tf_op | source)
XLA Modules:
  0.0 96.7 jit_solution(15068606544752167740)
XLA Ops:
  0.7 94.6 %contract.1 = bf16[2,4,32,2048]{3,2,1,0:T(8,128)(2,1)S(1)} custom-call(s32[1]{0:T(128)S(6)} %copy.8.source_ref, s32[2,2]{1,0:T(2,128)} %op_ref.1, s32[2,128]{1,0:T(2,128)} %listed_ref.1, s32[4,4,128]{2,1,0:T(4,128)} %bitcast.3, bf16[1,2,2048,256]{3,2,1,0:T(8,128)(2,1)} %peramb_ref.1, bf16[1,2,2,512,512]{4,3,2,1,0:T(8,128)(2,1)} %sink_ref.1, ...), custom_call_target="tpu_custom_call" | custom-call | tf_op jit(solution)/shard_map/contract/pallas_call | solution.py:323
  95.2 1.5 %reshape.7 = bf16[2,4,16,2,2048]{4,3,2,1,0:T(2,128)(2,1)} reshape(bf16[2,4,32,2048]{3,2,1,0:T(8,128)(2,1)S(1)} %contract.1) | data formatting | bytes 2097152 | tf_op jit(solution)/shard_map/reshape | solution.py:364

commit v3 on v2

--- a/solution.py
+++ b/solution.py
@@ -30,7 +30,7 @@
     source_ref, op_ref, listed_ref, slot_ref, peramb_ref, sink_ref, optab_ref, out_ref,
     perv, sinkv, lhs, sendb, recvb, tbl, hot, right,
     in_sem, a2a_send, a2a_recv, p1_send, p1_recv, hop_send, hop_recv, fw_send, fw_recv,
-    ready_y, ready_z, ready_x, ready_c,
+    ready_y, ready_b, ready_a, ready_c,
 ):
     nv = sinkv.shape[3]
     n_y = sendb.shape[1]
@@ -39,18 +39,25 @@
     sel = listed_ref.shape[1]
     n = SIDE
     half = n // 2
-    quarters = n // 2
     t = lax.axis_index("tpair")
     y = lax.axis_index("col")
     c = t % CORES
     x = (t // CORES) % n
     z = t // (CORES * n)
 
-    def at_z(i):
-        return ((((z + i) % n) * n + x) * CORES + c, y)
-
-    def at_x(i):
-        return ((z * n + (x + i) % n) * CORES + c, y)
+    a = (1 - c) * z + c * x
+    b = (1 - c) * x + c * z
+
+    def ring_id(a_, b_):
+        z_ = (1 - c) * a_ + c * b_
+        x_ = (1 - c) * b_ + c * a_
+        return ((z_ * n + x_) * CORES + c, y)
+
+    def first_axis(i):
+        return ring_id(a, (b + i) % n)
+
+    def second_axis(i):
+        return ring_id((a + i) % n, b)
 
     def at_y(i):
         return (t, (y + i) % n_y)
@@ -72,9 +79,9 @@
     for i in range(1, n_y):
         peers.append((at_y(i), y + i < n_y, ready_y.at[i], ready_y.at[n_y - i]))
     for i in range(1, n):
-        peers.append((at_z(i), z + i < n, ready_z.at[i], ready_z.at[n - i]))
+        peers.append((first_axis(i), b + i < n, ready_b.at[i], ready_b.at[n - i]))
     for i in (1, n - 1):
-        peers.append((at_x(i), x + i < n, ready_x.at[i], ready_x.at[n - i]))
+        peers.append((second_axis(i), a + i < n, ready_a.at[i], ready_a.at[n - i]))
     peers.append((partner, c == 1, ready_c.at[0], ready_c.at[0]))
     barrier = pltpu.get_barrier_semaphore()
     for dev, later, _, _ in peers:
@@ -85,9 +92,9 @@
 
     shard = optab_ref[...].astype(F32)
     for r in range(2):
-        tbl[z, x, c, r] = shard[:, r, :].astype(BF16)
-
-    earlier = y + z + (x + n - 1) // n + (x + 1) // n + 1 - c
+        tbl[c, a, b, r] = shard[:, r, :].astype(BF16)
+
+    earlier = y + b + (a + n - 1) // n + (a + 1) // n + 1 - c
 
     @pl.when(earlier > 0)
     def _():
@@ -108,17 +115,26 @@
 
     def shard_copy(i):
         return pltpu.make_async_remote_copy(
-            src_ref=tbl.at[z, x, c], dst_ref=tbl.at[z, x, c],
+            src_ref=tbl.at[c, a, b], dst_ref=tbl.at[c, a, b],
             send_sem=p1_send.at[i], recv_sem=p1_recv.at[i],
-            device_id=at_z(i), device_id_type=MESH,
+            device_id=first_axis(i), device_id_type=MESH,
         )
 
     phase1 = [None] + [shard_copy(i) for i in range(1, n)]
     for i in range(1, n):
 
-        @pl.when(z + i >= n)
+        @pl.when(b + i >= n)
         def _(i=i):
             phase1[i].start()
+
+    @pl.when(c == 0)
+    def _():
+        for i in range(1, n):
+
+            @pl.when(b + i < n)
+            def _(i=i):
+                pl.semaphore_wait(ready_b.at[i], 1)
+                phase1[i].start()
 
     row = lax.broadcasted_iota(jnp.int32, (2 * sel, sel), 0)
     col = lax.broadcasted_iota(jnp.int32, (2 * sel, sel), 1)
@@ -162,86 +178,94 @@
 
     for k in range(prods):
         pos = slot_ref[source_ref[0] * prods + op_ref[k, 1]]
+        pt = pos // 16
+        pc = pt % CORES
+        px = (pt // CORES) % n
+        pz = pt // (CORES * n)
+        pa = (1 - pc) * pz + pc * px
+        pb = (1 - pc) * px + pc * pz
+        idx = ((pc * n + pa) * n + pb) * 16 + pos % 16
         for j in range(nv // 128):
-            hot[pl.ds(k * nv + j * 128, 128), :] = onehot_rows(pos[j : j + 1, :], hot.shape[1])
+            hot[pl.ds(k * nv + j * 128, 128), :] = onehot_rows(idx[j : j + 1, :], hot.shape[1])
+
+    @pl.when(c == 1)
+    def _():
+        for i in range(1, n):
+
+            @pl.when(b + i < n)
+            def _(i=i):
+                pl.semaphore_wait(ready_b.at[i], 1)
+                phase1[i].start()
+
+    for cp in phase1[1:]:
+        cp.wait_recv()
 
     hops = {}
     forward = {}
 
-    def piece(q, d, st, block):
-        if st < half:
-            return tbl.at[pl.ds(2 * q, 2), block, c]
-        return tbl.at[pl.ds(2 * q + d, 1), block, c]
-
-    def hop(q, d, st):
-        part = piece(q, d, st, (x + n - st + 1) % n if d == 0 else (x + st - 1) % n)
+    def hop(d, st, h):
+        part = tbl.at[c, (a + n - st + 1) % n if d == 0 else (a + st - 1) % n, pl.ds(h * half, half)]
         cp = pltpu.make_async_remote_copy(
             src_ref=part, dst_ref=part,
-            send_sem=hop_send.at[q, d, st], recv_sem=hop_recv.at[q, d, st],
-            device_id=at_x(1 if d == 0 else n - 1), device_id_type=MESH,
+            send_sem=hop_send.at[d, st, h], recv_sem=hop_recv.at[d, st, h],
+            device_id=second_axis(1 if d == 0 else n - 1), device_id_type=MESH,
         )
         cp.start()
-        hops[q, d, st] = cp
-
-    def pass_on(q, d, st):
-        part = piece(q, d, st, (x + n - st) % n if d == 0 else (x + st) % n)
+        hops[d, st, h] = cp
+
+    def pass_on(d, st, h):
+        part = tbl.at[c, (a + n - st) % n if d == 0 else (a + st) % n, pl.ds(h * half, half)]
         cp = pltpu.make_async_remote_copy(
             src_ref=part, dst_ref=part,
-            send_sem=fw_send.at[q, d, st], recv_sem=fw_recv.at[q, d, st],
+            send_sem=fw_send.at[d, st, h], recv_sem=fw_recv.at[d, st, h],
             device_id=partner, device_id_type=MESH,
         )
         cp.start()
-        forward[q, d, st] = cp
-
-    def open_pair(q):
-        for w in (2 * q, 2 * q + 1):
-            for i in range(1, n):
-                if i <= w:
-
-                    @pl.when(z + i == w)
-                    def _(i=i):
-                        pl.semaphore_wait(ready_z.at[i], 1)
-                        phase1[i].start()
-
-        for w in (2 * q, 2 * q + 1):
-            for i in range(1, n):
-
-                @pl.when((w + i) % n == z)
-                def _(i=i):
-                    phase1[i].wait_recv()
-
-        if q == 0:
-            await_answer(n_y - 1 + n - 1)
-            await_answer(n_y - 1 + n)
+        forward[d, st, h] = cp
+
+    def relay(st):
+        for h in range(2):
+            for d in range(2):
+                if (d, st, h) in hops:
+                    hops[d, st, h].wait_recv()
+                    if st + 1 < half or (st + 1 == half and h == d):
+                        hop(d, st + 1, h)
+                    pass_on(d, st, h)
+
+    span = n * 16
+    width = nv // 2
+
+    def pick(st):
         for d in range(2):
-            hop(q, d, 1)
-        if q == 0:
-            await_answer(n_y - 1 + n + 1)
-        pass_on(q, 0, 0)
-
-    def relay(q, st):
-        for d in range(2):
-            hops[q, d, st].wait_recv()
-            if st < half:
-                hop(q, d, st + 1)
-            pass_on(q, d, st)
-
-    def pick(q):
-        for d in range(2):
-            for st in range(half + 1):
-                if (q, d, st) in forward:
-                    forward[q, d, st].wait_recv()
-        span = hot.shape[1] // quarters
-        width = nv // 2
+            for h in range(2):
+                if (d, st, h) in forward:
+                    forward[d, st, h].wait_recv()
+        blocks = []
+        for core, at in ((c, a), (1 - c, b)):
+            for i in (st, n - st) if 0 < st < half else (st,):
+                blocks.append((core, (at + i) % n))
+        pairs = [blocks[i : i + 2] for i in range(0, len(blocks), 2)]
 
         def column(j, carry):
             at = pl.ds(pl.multiple_of((j % 2) * width, width), width)
-            rows = tbl[2 * q : 2 * q + 2, :, :, j // 2, :, at].reshape(span, width)
-            got = jnp.dot(
-                hot[:, q * span : (q + 1) * span], rows, preferred_element_type=F32
-            ).astype(BF16).reshape(prods, nv, width)
+            got = None
+            for pair in pairs:
+                left = jnp.concatenate(
+                    [
+                        hot[:, pl.ds(pl.multiple_of((core * n + blk) * span, span), span)]
+                        for core, blk in pair
+                    ],
+                    axis=1,
+                )
+                rows = jnp.concatenate(
+                    [tbl[core, blk, :, j // 2, :, at].reshape(span, width) for core, blk in pair],
+                    axis=0,
+                )
+                part = jnp.dot(left, rows, preferred_element_type=F32)
+                got = part if got is None else got + part
+            got = got.astype(BF16).reshape(prods, nv, width)
             to = pl.ds(pl.multiple_of(j * width, width), width)
-            if q == 0:
+            if st == 0:
                 right[:, :, to] = got
             else:
                 right[:, :, to] = right[:, :, to] + got
@@ -249,30 +273,24 @@
 
         lax.fori_loop(0, 4, column, 0)
 
-    open_pair(0)
-    relay(0, 1)
-    relay(0, 2)
-    open_pair(1)
-    relay(0, 3)
-    relay(1, 1)
-    relay(0, 4)
-    relay(1, 2)
+    await_answer(n_y - 1 + n - 1)
+    for h in range(2):
+        hop(0, 1, h)
+    await_answer(n_y - 1 + n + 1)
+    for h in range(2):
+        pass_on(0, 0, h)
+    await_answer(n_y - 1 + n)
+    for h in range(2):
+        hop(1, 1, h)
+    relay(1)
     pick(0)
-    open_pair(2)
-    relay(1, 3)
-    relay(2, 1)
-    open_pair(3)
-    relay(1, 4)
-    relay(2, 2)
+    relay(2)
     pick(1)
-    relay(3, 1)
-    relay(2, 3)
-    relay(3, 2)
-    relay(2, 4)
+    relay(3)
     pick(2)
-    relay(3, 3)
-    relay(3, 4)
+    relay(4)
     pick(3)
+    pick(4)
 
     for cp in exchange:
         cp.wait_recv()
@@ -331,7 +349,7 @@
             pltpu.VMEM((n_y, prods, 2 * own, 2 * nv), BF16),
             pltpu.VMEM((NS, n_y, prods * 2 * own, cols), BF16),
             pltpu.VMEM((NS, n_y, prods * 2 * own, cols), BF16),
-            pltpu.VMEM((SIDE, SIDE, CORES, 2, shard, nv), BF16),
+            pltpu.VMEM((CORES, SIDE, SIDE, 2, shard, nv), BF16),
             pltpu.VMEM((prods * nv, slots), BF16),
             pltpu.VMEM((prods, nv, 2 * nv), BF16),
             dma((1 + 2 * NS,)),
@@ -339,10 +357,10 @@
             dma((NS, n_y)),
             dma((SIDE,)),
             dma((SIDE,)),
-            dma((half, 2, half + 1)),
-            dma((half, 2, half + 1)),
-            dma((half, 2, half + 1)),
-            dma((half, 2, half + 1)),
+            dma((2, half + 1, 2)),
+            dma((2, half + 1, 2)),
+            dma((2, half + 1, 2)),
+            dma((2, half + 1, 2)),
             pltpu.SemaphoreType.REGULAR((n_y,)),
             pltpu.SemaphoreType.REGULAR((SIDE,)),
             pltpu.SemaphoreType.REGULAR((SIDE,)),

time: 96.9 us -> 55.2 us (0.57)
  the two profiles are of different devices: /device:TPU:769 before, /device:TPU:113 now
where the time goes in v3:
time: 55.2 us; the launch traced here: 54.1 us
  Pallas kernels  52 us (94%)
  local copies, waits for them, and re-layouts  1.5 us (3%)
  between operations  0.66 us (1%)
    pallas_call x1, Pallas kernels, per_device(): pl.pallas_call(kernel, out_shape=pltpu.VMEM((prods, NS, 2 * own, order),...  52 us
    reshape x1, local copies, waits for them, and re-layouts, per_device(): return out.reshape(prods, NS, own, 2, order)  1.5 us

profile of v3, /device:TPU:113, one launch (start us, length us, event | category | flops | bytes accessed | tf_op | source)
XLA Modules:
  0.0 54.1 jit_solution(16547674173545836399)
XLA Ops:
  0.7 52.0 %contract.1 = bf16[2,4,32,2048]{3,2,1,0:T(8,128)(2,1)S(1)} custom-call(s32[1]{0:T(128)S(6)} %copy.8.source_ref, s32[2,2]{1,0:T(2,128)} %op_ref.1, s32[2,128]{1,0:T(2,128)} %listed_ref.1, s32[4,4,128]{2,1,0:T(4,128)} %bitcast.3, bf16[1,2,2048,256]{3,2,1,0:T(8,128)(2,1)} %peramb_ref.1, bf16[1,2,2,512,512]{4,3,2,1,0:T(8,128)(2,1)} %sink_ref.1, ...), custom_call_target="tpu_custom_call" | custom-call | tf_op jit(solution)/shard_map/contract/pallas_call | solution.py:341
  52.6 1.5 %reshape.7 = bf16[2,4,16,2,2048]{4,3,2,1,0:T(2,128)(2,1)} reshape(bf16[2,4,32,2048]{3,2,1,0:T(8,128)(2,1)S(1)} %contract.1) | data formatting | bytes 2097152 | tf_op jit(solution)/shard_map/reshape | solution.py:382

commit v4 on v3

--- a/solution.py
+++ b/solution.py
@@ -135,6 +135,26 @@
             def _(i=i):
                 pl.semaphore_wait(ready_b.at[i], 1)
                 phase1[i].start()
+
+    hops = {}
+    forward = {}
+
+    def hop(p, d, st):
+        part = tbl.at[c, (a + n - st + 1) % n if d == 0 else (a + st - 1) % n, (b + n - p) % n]
+        hops[p, d, st] = pltpu.make_async_remote_copy(
+            src_ref=part, dst_ref=part,
+            send_sem=hop_send.at[d, st, p], recv_sem=hop_recv.at[d, st, p],
+            device_id=second_axis(1 if d == 0 else n - 1), device_id_type=MESH,
+        )
+        return hops[p, d, st]
+
+    second_later = (a + 1 < n, a == 0)
+    for d in range(2):
+        cp = hop(0, d, 1)
+
+        @pl.when(jnp.logical_not(second_later[d]))
+        def _(cp=cp):
+            cp.start()
 
     row = lax.broadcasted_iota(jnp.int32, (2 * sel, sel), 0)
     col = lax.broadcasted_iota(jnp.int32, (2 * sel, sel), 1)
@@ -197,49 +217,48 @@
                 pl.semaphore_wait(ready_b.at[i], 1)
                 phase1[i].start()
 
-    for cp in phase1[1:]:
-        cp.wait_recv()
-
-    hops = {}
-    forward = {}
-
-    def hop(d, st, h):
-        part = tbl.at[c, (a + n - st + 1) % n if d == 0 else (a + st - 1) % n, pl.ds(h * half, half)]
+    def pass_on(p, d, st):
+        part = tbl.at[c, (a + n - st) % n if d == 0 else (a + st) % n, (b + n - p) % n]
         cp = pltpu.make_async_remote_copy(
             src_ref=part, dst_ref=part,
-            send_sem=hop_send.at[d, st, h], recv_sem=hop_recv.at[d, st, h],
-            device_id=second_axis(1 if d == 0 else n - 1), device_id_type=MESH,
-        )
-        cp.start()
-        hops[d, st, h] = cp
-
-    def pass_on(d, st, h):
-        part = tbl.at[c, (a + n - st) % n if d == 0 else (a + st) % n, pl.ds(h * half, half)]
-        cp = pltpu.make_async_remote_copy(
-            src_ref=part, dst_ref=part,
-            send_sem=fw_send.at[d, st, h], recv_sem=fw_recv.at[d, st, h],
+            send_sem=fw_send.at[d, st, p], recv_sem=fw_recv.at[d, st, p],
             device_id=partner, device_id_type=MESH,
         )
         cp.start()
-        forward[d, st, h] = cp
-
-    def relay(st):
-        for h in range(2):
+        forward[p, d, st] = cp
+
+    def enter(p):
+        if p > 0:
+            phase1[p].wait_recv()
+            hop(p, 0, 1).start()
+            hop(p, 1, 1).start()
+        else:
             for d in range(2):
-                if (d, st, h) in hops:
-                    hops[d, st, h].wait_recv()
-                    if st + 1 < half or (st + 1 == half and h == d):
-                        hop(d, st + 1, h)
-                    pass_on(d, st, h)
+
+                @pl.when(second_later[d])
+                def _(d=d):
+                    pl.semaphore_wait(ready_a.at[1 if d == 0 else n - 1], 1)
+                    hops[0, d, 1].start()
+
+            await_answer(len(peers) - 1)
+        pass_on(p, 0, 0)
+
+    def relay(p, st):
+        for d in range(2):
+            if (p, d, st) in hops:
+                hops[p, d, st].wait_recv()
+                if st + 1 < half or (st + 1 == half and d == p % 2):
+                    hop(p, d, st + 1).start()
+                pass_on(p, d, st)
 
     span = n * 16
     width = nv // 2
 
     def pick(st):
-        for d in range(2):
-            for h in range(2):
-                if (d, st, h) in forward:
-                    forward[d, st, h].wait_recv()
+        for p in range(n):
+            for d in range(2):
+                if (p, d, st) in forward:
+                    forward[p, d, st].wait_recv()
         blocks = []
         for core, at in ((c, a), (1 - c, b)):
             for i in (st, n - st) if 0 < st < half else (st,):
@@ -273,24 +292,17 @@
 
         lax.fori_loop(0, 4, column, 0)
 
-    await_answer(n_y - 1 + n - 1)
-    for h in range(2):
-        hop(0, 1, h)
-    await_answer(n_y - 1 + n + 1)
-    for h in range(2):
-        pass_on(0, 0, h)
-    await_answer(n_y - 1 + n)
-    for h in range(2):
-        hop(1, 1, h)
-    relay(1)
-    pick(0)
-    relay(2)
-    pick(1)
-    relay(3)
-    pick(2)
-    relay(4)
-    pick(3)
-    pick(4)
+    arrival = [min(p, n - p) for p in range(n)]
+    steps = []
+    for p in range(n):
+        start = 0.5 * (arrival[p] + 1) if p else 0.0
+        steps.append((start, 0, p, enter, (p,)))
+        for st in range(1, half + 1):
+            steps.append((start + st, st, p, relay, (p, st)))
+    for st in range(half + 1):
+        steps.append((3.2 + st, half + 1, st, pick, (st,)))
+    for _, _, _, act, args in sorted(steps, key=lambda step: step[:3]):
+        act(*args)
 
     for cp in exchange:
         cp.wait_recv()
@@ -357,10 +369,10 @@
             dma((NS, n_y)),
             dma((SIDE,)),
             dma((SIDE,)),
-            dma((2, half + 1, 2)),
-            dma((2, half + 1, 2)),
-            dma((2, half + 1, 2)),
-            dma((2, half + 1, 2)),
+            dma((2, half + 1, SIDE)),
+            dma((2, half + 1, SIDE)),
+            dma((2, half + 1, SIDE)),
+            dma((2, half + 1, SIDE)),
             pltpu.SemaphoreType.REGULAR((n_y,)),
             pltpu.SemaphoreType.REGULAR((SIDE,)),
             pltpu.SemaphoreType.REGULAR((SIDE,)),

time: 55.2 us -> 59.2 us (1.072); the launches traced: 54.1 us -> 59 us
  Pallas kernels: 52 us -> 56.8 us
    pallas_call x1, Pallas kernels: 52 us -> 56.8 us  [per_device(): pl.pallas_call(kernel, out_shape=pltpu.VMEM((prods, NS, 2 * own, order),...]
where the time goes in v4:
time: 59.2 us; the launch traced here: 59 us
  Pallas kernels  56.8 us (96%)
  local copies, waits for them, and re-layouts  1.5 us (3%)
  between operations  0.66 us (1%)
    pallas_call x1, Pallas kernels, per_device(): pl.pallas_call(kernel, out_shape=pltpu.VMEM((prods, NS, 2 * own, order),...  56.8 us
    reshape x1, local copies, waits for them, and re-layouts, per_device(): return out.reshape(prods, NS, own, 2, order)  1.5 us

profile of v4, /device:TPU:113, one launch (start us, length us, event | category | flops | bytes accessed | tf_op | source)
XLA Modules:
  0.0 59.0 jit_solution(10919163413840029016)
XLA Ops:
  0.7 56.8 %contract.1 = bf16[2,4,32,2048]{3,2,1,0:T(8,128)(2,1)S(1)} custom-call(s32[1]{0:T(128)S(6)} %copy.8.source_ref, s32[2,2]{1,0:T(2,128)} %op_ref.1, s32[2,128]{1,0:T(2,128)} %listed_ref.1, s32[4,4,128]{2,1,0:T(4,128)} %bitcast.3, bf16[1,2,2048,256]{3,2,1,0:T(8,128)(2,1)} %peramb_ref.1, bf16[1,2,2,512,512]{4,3,2,1,0:T(8,128)(2,1)} %sink_ref.1, ...), custom_call_target="tpu_custom_call" | custom-call | tf_op jit(solution)/shard_map/contract/pallas_call | solution.py:353
  57.5 1.5 %reshape.7 = bf16[2,4,16,2,2048]{4,3,2,1,0:T(2,128)(2,1)} reshape(bf16[2,4,32,2048]{3,2,1,0:T(8,128)(2,1)S(1)} %contract.1) | data formatting | bytes 2097152 | tf_op jit(solution)/shard_map/reshape | solution.py:394

commit v5 on v3

--- a/solution.py
+++ b/solution.py
@@ -27,8 +27,8 @@
 
 
 def kernel(
-    source_ref, op_ref, listed_ref, slot_ref, peramb_ref, sink_ref, optab_ref, out_ref,
-    perv, sinkv, lhs, sendb, recvb, tbl, hot, right,
+    source_ref, op_ref, listed_hbm, slot_hbm, peramb_ref, sink_ref, optab_hbm, out_ref,
+    listed_ref, slot_ref, optab_ref, perv, sinkv, lhs, sendb, recvb, tbl, hot, right,
     in_sem, a2a_send, a2a_recv, p1_send, p1_recv, hop_send, hop_recv, fw_send, fw_recv,
     ready_y, ready_b, ready_a, ready_c,
 ):
@@ -36,7 +36,7 @@
     n_y = sendb.shape[1]
     own = sendb.shape[2] // (2 * CORES)
     prods = op_ref.shape[0]
-    sel = listed_ref.shape[1]
+    sel = listed_hbm.shape[1]
     n = SIDE
     half = n // 2
     t = lax.axis_index("tpair")
@@ -72,7 +72,13 @@
                     peramb_ref.at[0, r, pl.ds(s * nv, nv)], perv.at[s, r], in_sem.at[1 + s * 2 + r]
                 )
             )
-    for cp in loads:
+    small = [
+        pltpu.make_async_copy(src, dst, in_sem.at[len(loads) + i])
+        for i, (src, dst) in enumerate(
+            ((optab_hbm, optab_ref), (listed_hbm, listed_ref), (slot_hbm, slot_ref))
+        )
+    ]
+    for cp in small + loads:
         cp.start()
 
     peers = []
@@ -90,6 +96,7 @@
         def _(dev=dev):
             pl.semaphore_signal(barrier, inc=1, device_id=dev, device_id_type=MESH)
 
+    small[0].wait()
     shard = optab_ref[...].astype(F32)
     for r in range(2):
         tbl[c, a, b, r] = shard[:, r, :].astype(BF16)
@@ -121,7 +128,8 @@
         )
 
     phase1 = [None] + [shard_copy(i) for i in range(1, n)]
-    for i in range(1, n):
+    far_first = sorted(range(1, n), key=lambda i: -min(i, n - i))
+    for i in far_first:
 
         @pl.when(b + i >= n)
         def _(i=i):
@@ -129,7 +137,7 @@
 
     @pl.when(c == 0)
     def _():
-        for i in range(1, n):
+        for i in far_first:
 
             @pl.when(b + i < n)
             def _(i=i):
@@ -142,6 +150,7 @@
     odd = (row == 2 * col + 1).astype(F32)
     spread_a = jnp.concatenate([even, odd], axis=1).astype(BF16)
     spread_b = jnp.concatenate([odd, -even], axis=1).astype(BF16)
+    small[1].wait()
     hots = [onehot_rows(listed_ref[k : k + 1, :], nv) for k in range(prods)]
     loads[0].wait()
     for k in range(prods):
@@ -176,6 +185,16 @@
             cp.start()
             exchange.append(cp)
 
+    @pl.when(c == 1)
+    def _():
+        for i in range(1, n):
+
+            @pl.when(b + i < n)
+            def _(i=i):
+                pl.semaphore_wait(ready_b.at[i], 1)
+                phase1[i].start()
+
+    small[2].wait()
     for k in range(prods):
         pos = slot_ref[source_ref[0] * prods + op_ref[k, 1]]
         pt = pos // 16
@@ -188,15 +207,6 @@
         for j in range(nv // 128):
             hot[pl.ds(k * nv + j * 128, 128), :] = onehot_rows(idx[j : j + 1, :], hot.shape[1])
 
-    @pl.when(c == 1)
-    def _():
-        for i in range(1, n):
-
-            @pl.when(b + i < n)
-            def _(i=i):
-                pl.semaphore_wait(ready_b.at[i], 1)
-                phase1[i].start()
-
     for cp in phase1[1:]:
         cp.wait_recv()
 
@@ -212,6 +222,15 @@
         )
         cp.start()
         hops[d, st, h] = cp
+        if st == half:
+            near, col_y = second_axis(1 if d == 0 else n - 1)
+            cp = pltpu.make_async_remote_copy(
+                src_ref=part, dst_ref=part,
+                send_sem=fw_send.at[d, st, h], recv_sem=fw_recv.at[d, st, h],
+                device_id=(near + 1 - 2 * c, col_y), device_id_type=MESH,
+            )
+            cp.start()
+            forward[d, st, h] = cp
 
     def pass_on(d, st, h):
         part = tbl.at[c, (a + n - st) % n if d == 0 else (a + st) % n, pl.ds(h * half, half)]
@@ -230,7 +249,8 @@
                     hops[d, st, h].wait_recv()
                     if st + 1 < half or (st + 1 == half and h == d):
                         hop(d, st + 1, h)
-                    pass_on(d, st, h)
+                    if st < half:
+                        pass_on(d, st, h)
 
     span = n * 16
     width = nv // 2
@@ -341,9 +361,12 @@
     out = pl.pallas_call(
         kernel,
         out_shape=pltpu.VMEM((prods, NS, 2 * own, order), BF16),
-        in_specs=[smem, smem, vmem, vmem, hbm, hbm, vmem],
+        in_specs=[smem, smem, hbm, hbm, hbm, hbm, hbm],
         out_specs=vmem,
         scratch_shapes=[
+            pltpu.VMEM(listed_rows.shape, jnp.int32),
+            pltpu.VMEM((row_slot.shape[0] // nv, nv // 128, 128), jnp.int32),
+            pltpu.VMEM(op_table.shape, BF16),
             pltpu.VMEM((NS, 2, nv, cols), BF16),
             pltpu.VMEM(sink_ops.shape[1:], BF16),
             pltpu.VMEM((n_y, prods, 2 * own, 2 * nv), BF16),
@@ -352,7 +375,7 @@
             pltpu.VMEM((CORES, SIDE, SIDE, 2, shard, nv), BF16),
             pltpu.VMEM((prods * nv, slots), BF16),
             pltpu.VMEM((prods, nv, 2 * nv), BF16),
-            dma((1 + 2 * NS,)),
+            dma((4 + 2 * NS,)),
             dma((NS, n_y)),
             dma((NS, n_y)),
             dma((SIDE,)),

time: 55.2 us -> 55.1 us (level)
  the two profiles are of different devices: /device:TPU:113 before, /device:TPU:126 now
where the time goes in v5:
time: 55.1 us; the launch traced here: 54.9 us
  Pallas kernels  52.8 us (96%)
  local copies, waits for them, and re-layouts  1.5 us (3%)
  between operations  0.66 us (1%)
    pallas_call x1, Pallas kernels, per_device(): pl.pallas_call(kernel, out_shape=pltpu.VMEM((prods, NS, 2 * own, order),...  52.8 us
    reshape x1, local copies, waits for them, and re-layouts, per_device(): return out.reshape(prods, NS, own, 2, order)  1.5 us

profile of v5, /device:TPU:126, one launch (start us, length us, event | category | flops | bytes accessed | tf_op | source)
XLA Modules:
  0.0 54.9 jit_solution(10777383140317213517)
XLA Ops:
  0.7 52.8 %contract.1 = bf16[2,4,32,2048]{3,2,1,0:T(8,128)(2,1)S(1)} custom-call(s32[1]{0:T(128)S(6)} %copy.8.source_ref, s32[2,2]{1,0:T(2,128)} %op_ref.1, s32[2,128]{1,0:T(2,128)} %listed_hbm.1, s32[4,4,128]{2,1,0:T(4,128)} %bitcast.3, bf16[1,2,2048,256]{3,2,1,0:T(8,128)(2,1)} %peramb_ref.1, bf16[1,2,2,512,512]{4,3,2,1,0:T(8,128)(2,1)} %sink_ref.1, ...), custom_call_target="tpu_custom_call" | custom-call | tf_op jit(solution)/shard_map/contract/pallas_call | solution.py:361
  53.4 1.5 %reshape.7 = bf16[2,4,16,2,2048]{4,3,2,1,0:T(2,128)(2,1)} reshape(bf16[2,4,32,2048]{3,2,1,0:T(8,128)(2,1)S(1)} %contract.1) | data formatting | bytes 2097152 | tf_op jit(solution)/shard_map/reshape | solution.py:405

commit v6 on v5

--- a/solution.py
+++ b/solution.py
@@ -253,7 +253,7 @@
                         pass_on(d, st, h)
 
     span = n * 16
-    width = nv // 2
+    width = nv
 
     def pick(st):
         for d in range(2):
@@ -267,7 +267,6 @@
         pairs = [blocks[i : i + 2] for i in range(0, len(blocks), 2)]
 
         def column(j, carry):
-            at = pl.ds(pl.multiple_of((j % 2) * width, width), width)
             got = None
             for pair in pairs:
                 left = jnp.concatenate(
@@ -278,7 +277,7 @@
                     axis=1,
                 )
                 rows = jnp.concatenate(
-                    [tbl[core, blk, :, j // 2, :, at].reshape(span, width) for core, blk in pair],
+                    [tbl[core, blk, :, j].reshape(span, width) for core, blk in pair],
                     axis=0,
                 )
                 part = jnp.dot(left, rows, preferred_element_type=F32)
@@ -291,7 +290,7 @@
                 right[:, :, to] = right[:, :, to] + got
             return carry
 
-        lax.fori_loop(0, 4, column, 0)
+        lax.fori_loop(0, 2, column, 0)
 
     await_answer(n_y - 1 + n - 1)
     for h in range(2):
@@ -308,8 +307,8 @@
     pick(1)
     relay(3)
     pick(2)
+    pick(3)
     relay(4)
-    pick(3)
     pick(4)
 
     for cp in exchange:

time: 55.1 us -> 53.9 us (0.978)
  the two profiles are of different devices: /device:TPU:126 before, /device:TPU:113 now
where the time goes in v6:
time: 53.9 us; the launch traced here: 53.1 us
  Pallas kernels  50.9 us (94%)
  local copies, waits for them, and re-layouts  1.5 us (3%)
  between operations  0.66 us (1%)
    pallas_call x1, Pallas kernels, per_device(): pl.pallas_call(kernel, out_shape=pltpu.VMEM((prods, NS, 2 * own, order),...  50.9 us
    reshape x1, local copies, waits for them, and re-layouts, per_device(): return out.reshape(prods, NS, own, 2, order)  1.5 us

profile of v6, /device:TPU:113, one launch (start us, length us, event | category | flops | bytes accessed | tf_op | source)
XLA Modules:
  0.0 53.1 jit_solution(10980699417292747870)
XLA Ops:
  0.7 50.9 %contract.1 = bf16[2,4,32,2048]{3,2,1,0:T(8,128)(2,1)S(1)} custom-call(s32[1]{0:T(128)S(6)} %copy.8.source_ref, s32[2,2]{1,0:T(2,128)} %op_ref.1, s32[2,128]{1,0:T(2,128)} %listed_hbm.1, s32[4,4,128]{2,1,0:T(4,128)} %bitcast.3, bf16[1,2,2048,256]{3,2,1,0:T(8,128)(2,1)} %peramb_ref.1, bf16[1,2,2,512,512]{4,3,2,1,0:T(8,128)(2,1)} %sink_ref.1, ...), custom_call_target="tpu_custom_call" | custom-call | tf_op jit(solution)/shard_map/contract/pallas_call | solution.py:360
  51.6 1.5 %reshape.7 = bf16[2,4,16,2,2048]{4,3,2,1,0:T(2,128)(2,1)} reshape(bf16[2,4,32,2048]{3,2,1,0:T(8,128)(2,1)S(1)} %contract.1) | data formatting | bytes 2097152 | tf_op jit(solution)/shard_map/reshape | solution.py:404
